TPU v7x, 256 devices: a whole 4x4x8 slice. The times are simulated.
256 devices in a mesh: blk: 8 (over x, y_hi), tile: 32 (over z, y_lo, core).
Axes of the slice: x: 4, y: 4 (y_hi: 2, y_lo: 2; y = y_hi * 2 + y_lo), z: 8, core: 2. Of those that a mesh axis runs over, the one named last changes fastest.
Arguments:
- grid_feat: bfloat16 [65536, 512], P(('blk', 'tile')), may hold values from -18 to 18
- queries: bfloat16 [65536, 512], P(('blk', 'tile')), may hold values from -90 to 90
- obs_keys: bfloat16 [2048, 512], P(('blk', 'tile')), may hold values from -4 to 4
- obs_values: bfloat16 [2048, 512], P(('blk', 'tile')), may hold values from -6 to 6
- block_mask: int32 [512, 16], P(('blk', 'tile')), may hold values from 0 to 1, as said below
- obs_valid: int32 [16], replicated, may hold values from 2 to 128, as said below
- out_weight: bfloat16 [512, 512], replicated, may hold values from -0.25 to 0.25
- conv_weight: bfloat16 [3, 3, 512, 512], replicated, may hold values from -0.09375 to 0.09375
Outputs:
- layer_out: bfloat16 [65536, 512], P(('blk', 'tile'))
Inputs may be any that keep to these rules, and one draw needn't show every extreme that they name: `block_mask`: row t has a 1 in column t mod 16. `obs_valid`: at least one entry equals 128.
All inputs are finite; a program needn't handle non-finite values.
Results may differ from a plain program's by a relative error of at most 0.007.
Values may be sent and summed in bfloat16 or wider, within the bound.
A program may use at most 64 MiB of HBM per device.

v0:
```python
import jax
import jax.numpy as jnp
from jax import lax
from jax.sharding import PartitionSpec as P

HEADS = 8
OBS_BLOCK = 128


def passed_along(array, axis, by):
    peers = lax.axis_size(axis)
    return lax.ppermute(array, axis, [(i, (i + by) % peers) for i in range(peers)])


def with_halo(block, sides, width):
    for axis, dim in sides:
        count = lax.axis_size(axis)
        forward = [(i, i + 1) for i in range(count - 1)]
        backward = [(target, source) for source, target in forward]
        low = lax.ppermute(
            lax.slice_in_dim(block, block.shape[dim] - width, None, axis=dim), axis, forward
        )
        high = lax.ppermute(lax.slice_in_dim(block, 0, width, axis=dim), axis, backward)
        block = jnp.concatenate([low, block, high], axis=dim)
    return block


def circulate(block, visit, carry):
    home = lax.axis_index("blk")
    count = lax.axis_size("blk")
    carry = visit(carry, block, home)
    for step in range(1, count):
        block = passed_along(block, "blk", 1)
        carry = visit(carry, block, (home - step) % count)
    return carry


def on_device(
    grid_feat, queries, obs_keys, obs_values, block_mask, obs_valid, out_weight, conv_weight
):
    q_dev, width = queries.shape
    head = width // HEADS
    scale = head ** (-0.5)
    tiles = block_mask.shape[0]
    nblocks = block_mask.shape[1]
    lon = q_dev // tiles
    group_rows = obs_keys.shape[0] * lax.axis_size("tile")
    query_heads = queries.reshape(q_dev, HEADS, head)
    mask_float = block_mask.astype(jnp.float32)
    block_ids = jnp.arange(nblocks, dtype=jnp.int32)

    def attend(carry, kv_rows, start):
        rows = kv_rows.shape[1]
        key_index = start + jnp.arange(rows, dtype=jnp.int32)
        member = (key_index // OBS_BLOCK)[:, None] == block_ids[None, :]
        limits = jnp.sum(jnp.where(member, obs_valid[None, :], 0), axis=1)
        live = key_index % OBS_BLOCK < limits
        wanted = (
            jnp.dot(mask_float, member.astype(jnp.float32).T, precision=lax.Precision.HIGHEST) > 0.5
        )
        allowed = wanted & live[None, :]
        top, total, acc = carry
        keys = kv_rows[0].reshape(rows, HEADS, head)
        values = kv_rows[1].reshape(rows, HEADS, head)
        scores = (
            jnp.einsum("qhd,khd->hqk", query_heads, keys, preferred_element_type=jnp.float32)
            * scale
        )
        scores = scores.reshape(HEADS, tiles, lon, rows)
        scores = jnp.where(allowed[None, :, None, :], scores, -jnp.inf).reshape(HEADS, q_dev, rows)
        new_top = jnp.maximum(top, jnp.max(scores, axis=-1))
        factor = jnp.exp(top - new_top)
        weights = jnp.exp(scores - new_top[..., None])
        total = total * factor + jnp.sum(weights, axis=-1)
        acc = acc * factor[..., None] + jnp.einsum(
            "hqk,khd->hqd", weights.astype(jnp.bfloat16), values, preferred_element_type=jnp.float32
        )
        return (new_top, total, acc)

    start_state = (
        jnp.full((HEADS, q_dev), -1e30, jnp.float32),
        jnp.zeros((HEADS, q_dev), jnp.float32),
        jnp.zeros((HEADS, q_dev, head), jnp.float32),
    )
    kv_local = jnp.stack([obs_keys, obs_values])

    def visit_shards(carry, block, owner):
        collected = lax.all_gather(block, "tile", axis=1, tiled=True)
        return attend(carry, collected, owner * group_rows)

    state = circulate(kv_local, visit_shards, start_state)
    top, total, acc = state
    mixed = (
        jnp.transpose(acc / total[..., None], (1, 0, 2)).reshape(q_dev, width).astype(jnp.bfloat16)
    )
    projected = jnp.dot(mixed, out_weight, preferred_element_type=jnp.float32)
    hidden = lax.optimization_barrier(
        (grid_feat.astype(jnp.float32) + projected).astype(jnp.bfloat16)
    )
    wide = hidden.astype(jnp.float32)
    normed = (wide * lax.rsqrt(jnp.mean(wide * wide, axis=-1, keepdims=True) + 1e-06)).astype(
        jnp.bfloat16
    )
    field = normed.reshape(tiles, lon, width)
    padded = with_halo(field, ((("blk", "tile"), 0),), 1)
    summed = jnp.zeros((q_dev, width), jnp.float32)
    for lat_off in range(3):
        for lon_off in range(3):
            moved = jnp.roll(padded[lat_off : lat_off + tiles], 1 - lon_off, axis=1)
            summed = summed + jnp.dot(
                moved.reshape(q_dev, width),
                conv_weight[lat_off, lon_off],
                preferred_element_type=jnp.float32,
            )
    return (wide + summed).astype(jnp.bfloat16)


def solution(mesh):
    in_specs = (
        P(("blk", "tile"), None),
        P(("blk", "tile"), None),
        P(("blk", "tile"), None),
        P(("blk", "tile"), None),
        P(("blk", "tile"), None),
        P(),
        P(),
        P(),
    )
    out_specs = P(("blk", "tile"), None)
    return jax.shard_map(
        on_device, mesh=mesh, in_specs=in_specs, out_specs=out_specs, check_vma=False
    )
```

profile of v0, /device:TPU:1, one launch (start us, length us, event | category | flops | bytes accessed | tf_op | source)
XLA Modules:
  0.0 375.5 jit_solution(6822890569749922319)
XLA Ops:
  0.0 1.4 pad_maximum_fusion.6
  1.4 3.7 collective-permute-start
  5.1 38.9 %all_gather.24 = bf16[2,256,512]{2,1,0:T(8,128)(2,1)S(1)} all-gather(bf16[2,8,512]{2,1,0:T(8,128)(2,1)} %pad_maximum_fusion.6), channel_id=1, replica_groups=mesh['blk'=8,'tile'=32] {'tile'}, dimensions={1}, use_global_device_ids=true | all-gather | bytes 540672 | tf_op jit(solution)/shard_map/all_gather | solution.py:88
  44.2 1.1 copy.84
  49.3 1.4 fusion.43
  50.7 1.3 fusion.41
  60.4 32.3 %all_gather.25 = bf16[2,256,512]{2,1,0:T(8,128)(2,1)S(1)} all-gather(bf16[2,8,512]{2,1,0:T(8,128)(2,1)} %collective-permute-done), channel_id=1, replica_groups=mesh['blk'=8,'tile'=32] {'tile'}, dimensions={1}, use_global_device_ids=true | all-gather | bytes 540672 | tf_op jit(solution)/shard_map/all_gather | solution.py:88
  92.8 0.9 copy.88
  93.6 2.4 collective-permute-start.1
  96.0 2.8 fusion.161
  100.6 34.7 %all_gather.26 = bf16[2,256,512]{2,1,0:T(8,128)(2,1)S(1)} all-gather(bf16[2,8,512]{2,1,0:T(8,128)(2,1)S(1)} %collective-permute-done.1), channel_id=1, replica_groups=mesh['blk'=8,'tile'=32] {'tile'}, dimensions={1}, use_global_device_ids=true | all-gather | bytes 540672 | tf_op jit(solution)/shard_map/all_gather | solution.py:88
  137.0 3.4 fusion.160
  141.2 1.4 collective-permute-done.2
  143.2 33.1 %all_gather.27 = bf16[2,256,512]{2,1,0:T(8,128)(2,1)S(1)} all-gather(bf16[2,8,512]{2,1,0:T(8,128)(2,1)S(1)} %collective-permute-done.2), channel_id=1, replica_groups=mesh['blk'=8,'tile'=32] {'tile'}, dimensions={1}, use_global_device_ids=true | all-gather | bytes 540672 | tf_op jit(solution)/shard_map/all_gather | solution.py:88
  177.5 3.4 fusion.159
  181.8 1.9 collective-permute-done.3
  184.2 34.7 %all_gather.28 = bf16[2,256,512]{2,1,0:T(8,128)(2,1)S(1)} all-gather(bf16[2,8,512]{2,1,0:T(8,128)(2,1)S(1)} %collective-permute-done.3), channel_id=1, replica_groups=mesh['blk'=8,'tile'=32] {'tile'}, dimensions={1}, use_global_device_ids=true | all-gather | bytes 540672 | tf_op jit(solution)/shard_map/all_gather | solution.py:88
  219.8 2.9 fusion.158
  224.2 4.7 %collective-permute-done.4 = bf16[2,8,512]{2,1,0:T(8,128)(2,1)S(1)} collective-permute-done((bf16[2,8,512]{2,1,0:T(8,128)(2,1)S(1)}, bf16[2,8,512]{2,1,0:T(8,128)(2,1)S(1)}, u32[]{:S(2)}, u32[]{:S(2)}) %collective-permute-start.4) | collective-permute-done | bytes 16416 | tf_op jit(solution)/shard_map/ppermute | solution.py:12
  229.5 33.1 %all_gather.29 = bf16[2,256,512]{2,1,0:T(8,128)(2,1)S(1)} all-gather(bf16[2,8,512]{2,1,0:T(8,128)(2,1)S(1)} %collective-permute-done.4), channel_id=1, replica_groups=mesh['blk'=8,'tile'=32] {'tile'}, dimensions={1}, use_global_device_ids=true | all-gather | bytes 540672 | tf_op jit(solution)/shard_map/all_gather | solution.py:88
  263.5 3.5 fusion.157
  267.8 2.1 collective-permute-done.5
  270.5 34.7 %all_gather.30 = bf16[2,256,512]{2,1,0:T(8,128)(2,1)S(1)} all-gather(bf16[2,8,512]{2,1,0:T(8,128)(2,1)S(1)} %collective-permute-done.5), channel_id=1, replica_groups=mesh['blk'=8,'tile'=32] {'tile'}, dimensions={1}, use_global_device_ids=true | all-gather | bytes 540672 | tf_op jit(solution)/shard_map/all_gather | solution.py:88
  306.1 3.4 fusion.156
  310.3 2.2 collective-permute-done.6
  312.5 33.1 %all_gather.31 = bf16[2,256,512]{2,1,0:T(8,128)(2,1)S(1)} all-gather(bf16[2,8,512]{2,1,0:T(8,128)(2,1)S(1)} %collective-permute-done.6), channel_id=1, replica_groups=mesh['blk'=8,'tile'=32] {'tile'}, dimensions={1}, use_global_device_ids=true | all-gather | bytes 540672 | tf_op jit(solution)/shard_map/all_gather | solution.py:88
  346.7 1.6 fusion.155
  349.7 1.0 copy-done.2
  361.7 3.5 collective-permute-start.7
  365.2 1.9 collective-permute-start.8
  367.2 4.3 %collective-permute-done.8 = bf16[1,128,512]{2,1,0:T(8,128)(2,1)S(1)} collective-permute-done((bf16[1,128,512]{2,1,0:T(8,128)(2,1)S(1)}, bf16[1,128,512]{2,1,0:T(8,128)(2,1)S(1)}, u32[]{:S(2)}, u32[]{:S(2)}) %collective-permute-start.8) | collective-permute-done | bytes 131104 | tf_op jit(solution)/shard_map/ppermute | solution.py:23
  374.5 1.0 fusion.33
  (168 shorter events, 43.2 us)
Async XLA Ops:
  0.0 360.4 %copy-start = (bf16[512,512]{1,0:T(8,128)(2,1)S(1)}, bf16[512,512]{1,0:T(8,128)(2,1)}, u32[]{:S(2)}) copy-start(bf16[512,512]{1,0:T(8,128)(2,1)} %param.14) | copy-start | bytes 1572868
  1.4 59.0 %collective-permute-start = (bf16[2,8,512]{2,1,0:T(8,128)(2,1)}, bf16[2,8,512]{2,1,0:T(8,128)(2,1)}, u32[]{:S(2)}, u32[]{:S(2)}) collective-permute-start(bf16[2,8,512]{2,1,0:T(8,128)(2,1)} %pad_maximum_fusion.6), channel_id=1, source_target_pairs={{0,32},{32,64},{64,96},{96,128},{128,160},{160,192},{192,224},{224... | collective-permute-start | bytes 49160 | tf_op jit(solution)/shard_map/ppermute | solution.py:12
  93.6 6.4 %collective-permute-start.1 = (bf16[2,8,512]{2,1,0:T(8,128)(2,1)}, bf16[2,8,512]{2,1,0:T(8,128)(2,1)S(1)}, u32[]{:S(2)}, u32[]{:S(2)}) collective-permute-start(bf16[2,8,512]{2,1,0:T(8,128)(2,1)} %collective-permute-done), channel_id=1, source_target_pairs={{0,32},{32,64},{64,96},{96,128},{128,160},{160,192},{192,224},{224... | collective-permute-start | bytes 49160 | tf_op jit(solution)/shard_map/ppermute | solution.py:12
  136.2 6.4 %collective-permute-start.2 = (bf16[2,8,512]{2,1,0:T(8,128)(2,1)}, bf16[2,8,512]{2,1,0:T(8,128)(2,1)S(1)}, u32[]{:S(2)}, u32[]{:S(2)}) collective-permute-start(bf16[2,8,512]{2,1,0:T(8,128)(2,1)} %copy-done.25), channel_id=1, source_target_pairs={{0,32},{32,64},{64,96},{96,128},{128,160},{160,192},{192,224},{224... | collective-permute-start | bytes 49160 | tf_op jit(solution)/shard_map/ppermute | solution.py:12
  177.2 6.4 %collective-permute-start.3 = (bf16[2,8,512]{2,1,0:T(8,128)(2,1)}, bf16[2,8,512]{2,1,0:T(8,128)(2,1)S(1)}, u32[]{:S(2)}, u32[]{:S(2)}) collective-permute-start(bf16[2,8,512]{2,1,0:T(8,128)(2,1)} %copy-done.26), channel_id=1, source_target_pairs={{0,32},{32,64},{64,96},{96,128},{128,160},{160,192},{192,224},{224... | collective-permute-start | bytes 49160 | tf_op jit(solution)/shard_map/ppermute | solution.py:12
  219.8 2.9 copy-start.24
  219.8 2.9 copy-start.15
  219.8 2.9 copy-start.17
  222.7 6.2 %copy-start.19 = (f32[8,256]{1,0:T(8,128)}, f32[8,256]{1,0:T(8,128)S(1)}, u32[]{:S(2)}) copy-start(f32[8,256]{1,0:T(8,128)S(1)} %get-tuple-element.75) | copy-start | bytes 24580
  222.7 6.2 %collective-permute-start.4 = (bf16[2,8,512]{2,1,0:T(8,128)(2,1)S(1)}, bf16[2,8,512]{2,1,0:T(8,128)(2,1)S(1)}, u32[]{:S(2)}, u32[]{:S(2)}) collective-permute-start(bf16[2,8,512]{2,1,0:T(8,128)(2,1)S(1)} %copy-done.24), channel_id=1, source_target_pairs={{0,32},{32,64},{64,96},{96,128},{128,160},{160,192},{192,224},{224... | collective-permute-start | bytes 49160 | tf_op jit(solution)/shard_map/ppermute | solution.py:12
  263.5 6.4 %collective-permute-start.5 = (bf16[2,8,512]{2,1,0:T(8,128)(2,1)}, bf16[2,8,512]{2,1,0:T(8,128)(2,1)S(1)}, u32[]{:S(2)}, u32[]{:S(2)}) collective-permute-start(bf16[2,8,512]{2,1,0:T(8,128)(2,1)} %copy-done.28), channel_id=1, source_target_pairs={{0,32},{32,64},{64,96},{96,128},{128,160},{160,192},{192,224},{224... | collective-permute-start | bytes 49160 | tf_op jit(solution)/shard_map/ppermute | solution.py:12
  306.1 6.4 %collective-permute-start.6 = (bf16[2,8,512]{2,1,0:T(8,128)(2,1)}, bf16[2,8,512]{2,1,0:T(8,128)(2,1)S(1)}, u32[]{:S(2)}, u32[]{:S(2)}) collective-permute-start(bf16[2,8,512]{2,1,0:T(8,128)(2,1)} %copy-done.27), channel_id=1, source_target_pairs={{0,32},{32,64},{64,96},{96,128},{128,160},{160,192},{192,224},{224... | collective-permute-start | bytes 49160 | tf_op jit(solution)/shard_map/ppermute | solution.py:12
  345.7 2.6 copy-start.16
  346.7 2.7 copy-start.1
  349.1 1.6 copy-start.2
  349.4 2.0 copy-start.3
  350.7 1.7 copy-start.4
  351.4 1.7 copy-start.5
  352.4 1.7 copy-start.6
  354.2 0.7 copy-start.22
  354.2 1.0 copy-start.7
  354.5 1.2 copy-start.8
  355.7 1.0 copy-start.9
  356.1 1.0 copy-start.10
  357.1 1.0 copy-start.11
  357.6 1.0 copy-start.12
  358.5 1.0 copy-start.13
  359.5 12.6 %slice-start = ((s8[4718592]{0:T(1024)(128)(4,1)}), s8[4194304]{0:T(1024)(128)(4,1)S(1)}, s32[]{:S(2)}) async-start(s8[4718592]{0:T(1024)(128)(4,1)} %bitcast.311), calls=%async_computation | async-start | bytes 8388608
  359.9 1.2 copy-start.14
  361.1 10.9 %slice-start.1 = ((s8[4718592]{0:T(1024)(128)(4,1)}), s8[524288]{0:T(1024)(128)(4,1)S(1)}, s32[]{:S(2)}) async-start(s8[4718592]{0:T(1024)(128)(4,1)} %bitcast.311), calls=%async_computation.1 | async-start | bytes 1048576
  361.7 5.4 %collective-permute-start.7 = (bf16[1,128,512]{2,1,0:T(8,128)(2,1)S(1)}, bf16[1,128,512]{2,1,0:T(8,128)(2,1)S(1)}, u32[]{:S(2)}, u32[]{:S(2)}) collective-permute-start(bf16[1,128,512]{2,1,0:T(8,128)(2,1)S(1)} %get-tuple-element.63), channel_id=1, source_target_pairs={{0,1},{1,2},{2,3},{3,4},{4,5},{5,6},{6,7},{7,8},{8,9},{9,10},{10,1... | collective-permute-start | bytes 393224 | tf_op jit(solution)/shard_map/ppermute | solution.py:20
  365.2 6.3 %collective-permute-start.8 = (bf16[1,128,512]{2,1,0:T(8,128)(2,1)S(1)}, bf16[1,128,512]{2,1,0:T(8,128)(2,1)S(1)}, u32[]{:S(2)}, u32[]{:S(2)}) collective-permute-start(bf16[1,128,512]{2,1,0:T(8,128)(2,1)S(1)} %get-tuple-element.62), channel_id=1, source_target_pairs={{1,0},{2,1},{3,2},{4,3},{5,4},{6,5},{7,6},{8,7},{9,8},{10,9},{11,1... | collective-permute-start | bytes 393224 | tf_op jit(solution)/shard_map/ppermute | solution.py:23
  (9 other events, 5.9 us)
where the time goes:
time: 376 us
  blocking collectives  275 us (73%)
  matrix products  35.6 us (9%)
  local copies, waits for them, and re-layouts  28 us (7%)
  waiting for transfers between devices  17.1 us (5%)
  starting transfers between devices  12.6 us (3%)
  other arithmetic  6.82 us (2%)
    all_gather x8, blocking collectives, visit_shards(): collected = lax.all_gather(block, 'tile', axis=1, tiled=True)  275 us
    dot_general x8, matrix products, attend(): jnp.einsum('qhd,khd->hqk', query_heads, keys, preferred_element_type=jnp....  21.3 us
    ppermute x7, waiting for transfers between devices, passed_along(): lax.ppermute(array, axis, [(i, (i + by) % peers) for i in range(peers)])  12.8 us
    unnamed x65, local copies, waits for them, and re-layouts  9.9 us
  transfers between devices with their start and end apart: 9, of which 7 were waited for; matrix products, arithmetic and copies ran while one was open for 10% of the time, Pallas kernels for 0%

commit v1 on v0

--- a/solution.py
+++ b/solution.py
@@ -2,6 +2,7 @@
 import jax.numpy as jnp
 from jax import lax
 from jax.sharding import PartitionSpec as P
+from jax.lax import all_to_all, axis_size
 
 HEADS = 8
 OBS_BLOCK = 128
@@ -85,7 +86,8 @@
     kv_local = jnp.stack([obs_keys, obs_values])
 
     def visit_shards(carry, block, owner):
-        collected = lax.all_gather(block, "tile", axis=1, tiled=True)
+        f_now = jnp.stack([block] * axis_size("tile"), 0)
+        collected = jnp.concatenate(all_to_all(f_now, "tile", 0, 0), axis=1)
         return attend(carry, collected, owner * group_rows)
 
     state = circulate(kv_local, visit_shards, start_state)

time: 376 us -> 231 us (0.61)
  blocking collectives: 275 us -> 0 us
  starting transfers between devices: 12.6 us -> 70.7 us
  waiting for transfers between devices: 17.1 us -> 74.7 us
  local copies, waits for them, and re-layouts: 28 us -> 49.6 us
  matrix products: 35.6 us -> 27.9 us
    all_gather x8 -> x0, blocking collectives: 275 us -> none  [visit_shards(): collected = lax.all_gather(block, 'tile', axis=1, tiled=True)]
    all_to_all x0 -> x8, waiting for transfers between devices: none -> 56 us  [visit_shards(): collected = jnp.concatenate(all_to_all(f_now, 'tile', 0, 0), axis=1)]
    all_to_all x0 -> x8, starting transfers between devices: none -> 49 us  [visit_shards(): collected = jnp.concatenate(all_to_all(f_now, 'tile', 0, 0), axis=1)]
    another operation x0 -> x24, local copies, waits for them, and re-layouts: none -> 29.3 us  [the longest x8 13.7 us: attend(): keys = kv_rows[0].reshape(rows, HEADS, head)]
    ppermute x7, starting transfers between devices: 7.17 us -> 15.6 us  [passed_along(): lax.ppermute(array, axis, [(i, (i + by) % peers) for i in range(peers)])]
    slice x9 -> x0, local copies, waits for them, and re-layouts: 6.07 us -> none  [attend(): keys = kv_rows[0].reshape(rows, HEADS, head)]
    dot_general x8, matrix products: 6.87 us -> 1.02 us  [attend(): jnp.dot(mask_float, member.astype(jnp.float32).T, precision=lax.Precision...]
    unnamed x65 -> x51, local copies, waits for them, and re-layouts: 9.9 us -> 6.46 us
  transfers between devices with their start and end apart: 9 -> 17, of which waited for: 7 -> 13; matrix products, arithmetic and copies ran while one was open for 10% -> 23% of each run, Pallas kernels for 0% -> 0%
where the time goes in v1:
time: 231 us; the launch traced here: 228 us
  waiting for transfers between devices  74.7 us (32%)
  starting transfers between devices  70.7 us (31%)
  local copies, waits for them, and re-layouts  49.6 us (21%)
  matrix products  27.9 us (12%)
  other arithmetic  4.26 us (2%)
    all_to_all x8, waiting for transfers between devices, visit_shards(): collected = jnp.concatenate(all_to_all(f_now, 'tile', 0, 0), axis=1)  56 us
    all_to_all x8, starting transfers between devices, visit_shards(): collected = jnp.concatenate(all_to_all(f_now, 'tile', 0, 0), axis=1)  49 us
    dot_general x8, matrix products, attend(): jnp.einsum('qhd,khd->hqk', query_heads, keys, preferred_element_type=jnp....  19.6 us
    ppermute x7, starting transfers between devices, passed_along(): lax.ppermute(array, axis, [(i, (i + by) % peers) for i in range(peers)])  15.6 us
    ppermute x7, waiting for transfers between devices, passed_along(): lax.ppermute(array, axis, [(i, (i + by) % peers) for i in range(peers)])  14.4 us
    another operation x8, local copies, waits for them, and re-layouts, attend(): keys = kv_rows[0].reshape(rows, HEADS, head)  13.7 us
    slice x8, local copies, waits for them, and re-layouts, attend(): values = kv_rows[1].reshape(rows, HEADS, head)  8.64 us
    another operation x8, local copies, waits for them, and re-layouts, attend(): values = kv_rows[1].reshape(rows, HEADS, head)  7.82 us
  transfers between devices with their start and end apart: 17, of which 13 were waited for; matrix products, arithmetic and copies ran while one was open for 23% of the time, Pallas kernels for 0%

profile of v1, /device:TPU:1, one launch (start us, length us, event | category | flops | bytes accessed | tf_op | source)
XLA Modules:
  0.0 227.9 jit_solution(18233171363771840418)
XLA Ops:
  1.6 11.3 %all-to-all-start = ((bf16[32,2,8,512]{3,2,1,0:T(8,128)(2,1)}), bf16[32,2,8,512]{3,2,1,0:T(8,128)(2,1)S(1)}, u32[]{:S(2)}, u32[]{:S(2)}) async-start(bf16[32,2,8,512]{3,2,1,0:T(8,128)(2,1)} %stack.25), calls=%async_computation | async-start | bytes 1048576 | tf_op jit(solution)/shard_map/all_to_all | solution.py:90
  12.9 2.7 %collective-permute-start = (bf16[2,8,512]{2,1,0:T(8,128)(2,1)S(1)}, bf16[2,8,512]{2,1,0:T(8,128)(2,1)S(1)}, u32[]{:S(2)}, u32[]{:S(2)}) collective-permute-start(bf16[2,8,512]{2,1,0:T(8,128)(2,1)S(1)} %pad_maximum_fusion.6), channel_id=1, source_target_pairs={{0,32},{32,64},{64,96},{96,128},{128,160},{160,192},{192,224},{224... | collective-permute-start | bytes 49160 | tf_op jit(solution)/shard_map/ppermute | solution.py:13
  15.6 3.6 %collective-permute-done = bf16[2,8,512]{2,1,0:T(8,128)(2,1)S(1)} collective-permute-done((bf16[2,8,512]{2,1,0:T(8,128)(2,1)S(1)}, bf16[2,8,512]{2,1,0:T(8,128)(2,1)S(1)}, u32[]{:S(2)}, u32[]{:S(2)}) %collective-permute-start) | collective-permute-done | bytes 16416 | tf_op jit(solution)/shard_map/ppermute | solution.py:13
  19.3 10.4 %all-to-all-done = bf16[32,2,8,512]{3,2,1,0:T(8,128)(2,1)S(1)} async-done(((bf16[32,2,8,512]{3,2,1,0:T(8,128)(2,1)}), bf16[32,2,8,512]{3,2,1,0:T(8,128)(2,1)S(1)}, u32[]{:S(2)}, u32[]{:S(2)}) %all-to-all-start) | async-done | bytes 524320 | tf_op jit(solution)/shard_map/all_to_all | solution.py:90
  30.5 5.1 %all-to-all-start.1 = ((bf16[32,2,8,512]{3,2,1,0:T(8,128)(2,1)}), bf16[32,2,8,512]{3,2,1,0:T(8,128)(2,1)S(1)}, u32[]{:S(2)}, u32[]{:S(2)}) async-start(bf16[32,2,8,512]{3,2,1,0:T(8,128)(2,1)} %stack.26), calls=%async_computation.1 | async-start | bytes 1048576 | tf_op jit(solution)/shard_map/all_to_all | solution.py:90
  35.8 2.7 %collective-permute-start.1 = (bf16[2,8,512]{2,1,0:T(8,128)(2,1)S(1)}, bf16[2,8,512]{2,1,0:T(8,128)(2,1)S(1)}, u32[]{:S(2)}, u32[]{:S(2)}) collective-permute-start(bf16[2,8,512]{2,1,0:T(8,128)(2,1)S(1)} %collective-permute-done), channel_id=1, source_target_pairs={{0,32},{32,64},{64,96},{96,128},{128,160},{160,192},{192,224},{224... | collective-permute-start | bytes 49160 | tf_op jit(solution)/shard_map/ppermute | solution.py:13
  38.6 3.6 %collective-permute-done.1 = bf16[2,8,512]{2,1,0:T(8,128)(2,1)S(1)} collective-permute-done((bf16[2,8,512]{2,1,0:T(8,128)(2,1)S(1)}, bf16[2,8,512]{2,1,0:T(8,128)(2,1)S(1)}, u32[]{:S(2)}, u32[]{:S(2)}) %collective-permute-start.1) | collective-permute-done | bytes 16416 | tf_op jit(solution)/shard_map/ppermute | solution.py:13
  42.3 10.4 %all-to-all-done.1 = bf16[32,2,8,512]{3,2,1,0:T(8,128)(2,1)S(1)} async-done(((bf16[32,2,8,512]{3,2,1,0:T(8,128)(2,1)}), bf16[32,2,8,512]{3,2,1,0:T(8,128)(2,1)S(1)}, u32[]{:S(2)}, u32[]{:S(2)}) %all-to-all-start.1) | async-done | bytes 524320 | tf_op jit(solution)/shard_map/all_to_all | solution.py:90
  53.5 5.0 %all-to-all-start.2 = ((bf16[32,2,8,512]{3,2,1,0:T(8,128)(2,1)}), bf16[32,2,8,512]{3,2,1,0:T(8,128)(2,1)S(1)}, u32[]{:S(2)}, u32[]{:S(2)}) async-start(bf16[32,2,8,512]{3,2,1,0:T(8,128)(2,1)} %stack.27), calls=%async_computation.2 | async-start | bytes 1048576 | tf_op jit(solution)/shard_map/all_to_all | solution.py:90
  58.8 2.7 %collective-permute-start.2 = (bf16[2,8,512]{2,1,0:T(8,128)(2,1)S(1)}, bf16[2,8,512]{2,1,0:T(8,128)(2,1)S(1)}, u32[]{:S(2)}, u32[]{:S(2)}) collective-permute-start(bf16[2,8,512]{2,1,0:T(8,128)(2,1)S(1)} %collective-permute-done.1), channel_id=1, source_target_pairs={{0,32},{32,64},{64,96},{96,128},{128,160},{160,192},{192,224},{224... | collective-permute-start | bytes 49160 | tf_op jit(solution)/shard_map/ppermute | solution.py:13
  61.6 3.6 %collective-permute-done.2 = bf16[2,8,512]{2,1,0:T(8,128)(2,1)S(1)} collective-permute-done((bf16[2,8,512]{2,1,0:T(8,128)(2,1)S(1)}, bf16[2,8,512]{2,1,0:T(8,128)(2,1)S(1)}, u32[]{:S(2)}, u32[]{:S(2)}) %collective-permute-start.2) | collective-permute-done | bytes 16416 | tf_op jit(solution)/shard_map/ppermute | solution.py:13
  65.2 10.4 %all-to-all-done.2 = bf16[32,2,8,512]{3,2,1,0:T(8,128)(2,1)S(1)} async-done(((bf16[32,2,8,512]{3,2,1,0:T(8,128)(2,1)}), bf16[32,2,8,512]{3,2,1,0:T(8,128)(2,1)S(1)}, u32[]{:S(2)}, u32[]{:S(2)}) %all-to-all-start.2) | async-done | bytes 524320 | tf_op jit(solution)/shard_map/all_to_all | solution.py:90
  76.5 4.8 %all-to-all-start.3 = ((bf16[32,2,8,512]{3,2,1,0:T(8,128)(2,1)}), bf16[32,2,8,512]{3,2,1,0:T(8,128)(2,1)S(1)}, u32[]{:S(2)}, u32[]{:S(2)}) async-start(bf16[32,2,8,512]{3,2,1,0:T(8,128)(2,1)} %stack.28), calls=%async_computation.3 | async-start | bytes 1048576 | tf_op jit(solution)/shard_map/all_to_all | solution.py:90
  81.7 2.7 %collective-permute-start.3 = (bf16[2,8,512]{2,1,0:T(8,128)(2,1)S(1)}, bf16[2,8,512]{2,1,0:T(8,128)(2,1)S(1)}, u32[]{:S(2)}, u32[]{:S(2)}) collective-permute-start(bf16[2,8,512]{2,1,0:T(8,128)(2,1)S(1)} %collective-permute-done.2), channel_id=1, source_target_pairs={{0,32},{32,64},{64,96},{96,128},{128,160},{160,192},{192,224},{224... | collective-permute-start | bytes 49160 | tf_op jit(solution)/shard_map/ppermute | solution.py:13
  84.4 3.6 %collective-permute-done.3 = bf16[2,8,512]{2,1,0:T(8,128)(2,1)S(1)} collective-permute-done((bf16[2,8,512]{2,1,0:T(8,128)(2,1)S(1)}, bf16[2,8,512]{2,1,0:T(8,128)(2,1)S(1)}, u32[]{:S(2)}, u32[]{:S(2)}) %collective-permute-start.3) | collective-permute-done | bytes 16416 | tf_op jit(solution)/shard_map/ppermute | solution.py:13
  88.8 9.6 %all-to-all-done.3 = bf16[32,2,8,512]{3,2,1,0:T(8,128)(2,1)S(1)} async-done(((bf16[32,2,8,512]{3,2,1,0:T(8,128)(2,1)}), bf16[32,2,8,512]{3,2,1,0:T(8,128)(2,1)S(1)}, u32[]{:S(2)}, u32[]{:S(2)}) %all-to-all-start.3) | async-done | bytes 524320 | tf_op jit(solution)/shard_map/all_to_all | solution.py:90
  99.3 5.5 %all-to-all-start.4 = ((bf16[32,2,8,512]{3,2,1,0:T(8,128)(2,1)}), bf16[32,2,8,512]{3,2,1,0:T(8,128)(2,1)}, u32[]{:S(2)}, u32[]{:S(2)}) async-start(bf16[32,2,8,512]{3,2,1,0:T(8,128)(2,1)} %stack.29), calls=%async_computation.4 | async-start | bytes 1048576 | tf_op jit(solution)/shard_map/all_to_all | solution.py:90
  105.0 2.7 %collective-permute-start.5 = (bf16[2,8,512]{2,1,0:T(8,128)(2,1)S(1)}, bf16[2,8,512]{2,1,0:T(8,128)(2,1)S(1)}, u32[]{:S(2)}, u32[]{:S(2)}) collective-permute-start(bf16[2,8,512]{2,1,0:T(8,128)(2,1)S(1)} %collective-permute-done.4), channel_id=1, source_target_pairs={{0,32},{32,64},{64,96},{96,128},{128,160},{160,192},{192,224},{224... | collective-permute-start | bytes 49160 | tf_op jit(solution)/shard_map/ppermute | solution.py:13
  119.1 2.9 %all-to-all-done.4 = bf16[32,2,8,512]{3,2,1,0:T(8,128)(2,1)} async-done(((bf16[32,2,8,512]{3,2,1,0:T(8,128)(2,1)}), bf16[32,2,8,512]{3,2,1,0:T(8,128)(2,1)}, u32[]{:S(2)}, u32[]{:S(2)}) %all-to-all-start.4) | async-done | bytes 524320 | tf_op jit(solution)/shard_map/all_to_all | solution.py:90
  122.9 6.2 %all-to-all-start.5 = ((bf16[32,2,8,512]{3,2,1,0:T(8,128)(2,1)}), bf16[32,2,8,512]{3,2,1,0:T(8,128)(2,1)}, u32[]{:S(2)}, u32[]{:S(2)}) async-start(bf16[32,2,8,512]{3,2,1,0:T(8,128)(2,1)} %stack.30), calls=%async_computation.5 | async-start | bytes 1048576 | tf_op jit(solution)/shard_map/all_to_all | solution.py:90
  134.5 2.9 %fusion.176 = (f32[8,256]{1,0:T(8,128)S(1)}, f32[8,256,256]{1,2,0:T(8,128)}) fusion(bf16[256,8,64]{0,2,1:T(8,128)(2,1)} %bitcast.360, bf16[256,8,64]{2,1,0:T(8,128)(2,1)} %reshape_squeeze.52, pred[256,256]{0,1:T(8,128)(4,1)} %copy.116), kind=kOutput, calls=%fused_computation.326 | convolution fusion | flops 68679680 | bytes 2695168 | tf_op jit(solution)/shard_map/qhd,khd->hqk/dot_general | solution.py:67
  141.3 4.5 %all-to-all-done.5 = bf16[32,2,8,512]{3,2,1,0:T(8,128)(2,1)} async-done(((bf16[32,2,8,512]{3,2,1,0:T(8,128)(2,1)}), bf16[32,2,8,512]{3,2,1,0:T(8,128)(2,1)}, u32[]{:S(2)}, u32[]{:S(2)}) %all-to-all-start.5) | async-done | bytes 524320 | tf_op jit(solution)/shard_map/all_to_all | solution.py:90
  146.7 5.7 %all-to-all-start.6 = ((bf16[32,2,8,512]{3,2,1,0:T(8,128)(2,1)}), bf16[32,2,8,512]{3,2,1,0:T(8,128)(2,1)}, u32[]{:S(2)}, u32[]{:S(2)}) async-start(bf16[32,2,8,512]{3,2,1,0:T(8,128)(2,1)} %stack.31), calls=%async_computation.6 | async-start | bytes 1048576 | tf_op jit(solution)/shard_map/all_to_all | solution.py:90
  152.4 2.9 %fusion.175 = (f32[8,256]{1,0:T(8,128)S(1)}, f32[8,256,256]{1,2,0:T(8,128)}) fusion(bf16[256,8,64]{0,2,1:T(8,128)(2,1)} %bitcast.361, bf16[256,8,64]{2,1,0:T(8,128)(2,1)} %reshape_squeeze.54, pred[256,256]{0,1:T(8,128)(4,1)} %copy.120), kind=kOutput, calls=%fused_computation.325 | convolution fusion | flops 68679680 | bytes 2695168 | tf_op jit(solution)/shard_map/qhd,khd->hqk/dot_general | solution.py:67
  159.1 2.9 %fusion.174 = (f32[8,256]{1,0:T(8,128)S(1)}, f32[8,256,256]{1,2,0:T(8,128)}) fusion(bf16[256,8,64]{0,2,1:T(8,128)(2,1)} %bitcast.362, bf16[256,8,64]{2,1,0:T(8,128)(2,1)} %reshape_squeeze.56, pred[256,256]{0,1:T(8,128)(4,1)} %copy.124), kind=kOutput, calls=%fused_computation.324 | convolution fusion | flops 68679680 | bytes 2695168 | tf_op jit(solution)/shard_map/qhd,khd->hqk/dot_general | solution.py:67
  163.1 6.4 %all-to-all-done.6 = bf16[32,2,8,512]{3,2,1,0:T(8,128)(2,1)} async-done(((bf16[32,2,8,512]{3,2,1,0:T(8,128)(2,1)}), bf16[32,2,8,512]{3,2,1,0:T(8,128)(2,1)}, u32[]{:S(2)}, u32[]{:S(2)}) %all-to-all-start.6) | async-done | bytes 524320 | tf_op jit(solution)/shard_map/all_to_all | solution.py:90
  171.1 5.5 %all-to-all-start.7 = ((bf16[32,2,8,512]{3,2,1,0:T(8,128)(2,1)}), bf16[32,2,8,512]{3,2,1,0:T(8,128)(2,1)}, u32[]{:S(2)}, u32[]{:S(2)}) async-start(bf16[32,2,8,512]{3,2,1,0:T(8,128)(2,1)} %stack.32), calls=%async_computation.7 | async-start | bytes 1048576 | tf_op jit(solution)/shard_map/all_to_all | solution.py:90
  178.4 2.1 reshape_squeeze.58
  181.6 2.9 %fusion.173 = (f32[8,256]{1,0:T(8,128)S(1)}, f32[8,256,256]{1,2,0:T(8,128)}) fusion(bf16[256,8,64]{0,2,1:T(8,128)(2,1)} %bitcast.363, bf16[256,8,64]{2,1,0:T(8,128)(2,1)} %reshape_squeeze.58, pred[256,256]{0,1:T(8,128)(4,1)} %copy.128), kind=kOutput, calls=%fused_computation.323 | convolution fusion | flops 68679680 | bytes 2695168 | tf_op jit(solution)/shard_map/qhd,khd->hqk/dot_general | solution.py:67
  189.4 2.9 %fusion.172 = (f32[8,256]{1,0:T(8,128)S(1)}, f32[8,256,256]{1,2,0:T(8,128)}) fusion(bf16[256,8,64]{0,2,1:T(8,128)(2,1)} %bitcast.364, bf16[256,8,64]{2,1,0:T(8,128)(2,1)} %reshape_squeeze.60, pred[256,256]{0,1:T(8,128)(4,1)} %copy.132), kind=kOutput, calls=%fused_computation.322 | convolution fusion | flops 68679680 | bytes 2695168 | tf_op jit(solution)/shard_map/qhd,khd->hqk/dot_general | solution.py:67
  213.4 4.3 %collective-permute-start.7 = (bf16[1,128,512]{2,1,0:T(8,128)(2,1)S(1)}, bf16[1,128,512]{2,1,0:T(8,128)(2,1)S(1)}, u32[]{:S(2)}, u32[]{:S(2)}) collective-permute-start(bf16[1,128,512]{2,1,0:T(8,128)(2,1)S(1)} %get-tuple-element.63), channel_id=1, source_target_pairs={{0,1},{1,2},{2,3},{3,4},{4,5},{5,6},{6,7},{7,8},{8,9},{9,10},{10,1... | collective-permute-start | bytes 393224 | tf_op jit(solution)/shard_map/ppermute | solution.py:21
  219.6 4.3 %collective-permute-done.8 = bf16[1,128,512]{2,1,0:T(8,128)(2,1)S(1)} collective-permute-done((bf16[1,128,512]{2,1,0:T(8,128)(2,1)S(1)}, bf16[1,128,512]{2,1,0:T(8,128)(2,1)S(1)}, u32[]{:S(2)}, u32[]{:S(2)}) %collective-permute-start.8) | collective-permute-done | bytes 131104 | tf_op jit(solution)/shard_map/ppermute | solution.py:24
  (170 shorter events, 70.5 us)
Async XLA Ops:
  0.0 212.1 %copy-start = (bf16[512,512]{1,0:T(8,128)(2,1)S(1)}, bf16[512,512]{1,0:T(8,128)(2,1)}, u32[]{:S(2)}) copy-start(bf16[512,512]{1,0:T(8,128)(2,1)} %param.14) | copy-start | bytes 1572868
  0.0 38.5 %copy-start.21 = (s32[16]{0:T(128)S(1)}, s32[16]{0:T(128)}, u32[]{:S(2)}) copy-start(s32[16]{0:T(128)} %param.13) | copy-start | bytes 196
  1.6 56.9 %copy-start.22 = (s32[2,16]{1,0:T(2,128)S(1)}, s32[2,16]{1,0:T(2,128)}, u32[]{:S(2)}) copy-start(s32[2,16]{1,0:T(2,128)} %param.12) | copy-start | bytes 388
  1.6 28.0 %all-to-all-start = ((bf16[32,2,8,512]{3,2,1,0:T(8,128)(2,1)}), bf16[32,2,8,512]{3,2,1,0:T(8,128)(2,1)S(1)}, u32[]{:S(2)}, u32[]{:S(2)}) async-start(bf16[32,2,8,512]{3,2,1,0:T(8,128)(2,1)} %stack.25), calls=%async_computation | async-start | bytes 1048576 | tf_op jit(solution)/shard_map/all_to_all | solution.py:90
  12.9 6.3 %collective-permute-start = (bf16[2,8,512]{2,1,0:T(8,128)(2,1)S(1)}, bf16[2,8,512]{2,1,0:T(8,128)(2,1)S(1)}, u32[]{:S(2)}, u32[]{:S(2)}) collective-permute-start(bf16[2,8,512]{2,1,0:T(8,128)(2,1)S(1)} %pad_maximum_fusion.6), channel_id=1, source_target_pairs={{0,32},{32,64},{64,96},{96,128},{128,160},{160,192},{192,224},{224... | collective-permute-start | bytes 49160 | tf_op jit(solution)/shard_map/ppermute | solution.py:13
  30.5 22.2 %all-to-all-start.1 = ((bf16[32,2,8,512]{3,2,1,0:T(8,128)(2,1)}), bf16[32,2,8,512]{3,2,1,0:T(8,128)(2,1)S(1)}, u32[]{:S(2)}, u32[]{:S(2)}) async-start(bf16[32,2,8,512]{3,2,1,0:T(8,128)(2,1)} %stack.26), calls=%async_computation.1 | async-start | bytes 1048576 | tf_op jit(solution)/shard_map/all_to_all | solution.py:90
  35.8 6.4 %collective-permute-start.1 = (bf16[2,8,512]{2,1,0:T(8,128)(2,1)S(1)}, bf16[2,8,512]{2,1,0:T(8,128)(2,1)S(1)}, u32[]{:S(2)}, u32[]{:S(2)}) collective-permute-start(bf16[2,8,512]{2,1,0:T(8,128)(2,1)S(1)} %collective-permute-done), channel_id=1, source_target_pairs={{0,32},{32,64},{64,96},{96,128},{128,160},{160,192},{192,224},{224... | collective-permute-start | bytes 49160 | tf_op jit(solution)/shard_map/ppermute | solution.py:13
  53.5 54.5 %copy-start.19 = (bf16[256,512]{1,0:T(8,128)(2,1)S(1)}, bf16[256,512]{1,0:T(8,128)(2,1)}, u32[]{:S(2)}) copy-start(bf16[256,512]{1,0:T(8,128)(2,1)} %param.9) | copy-start | bytes 786436
  53.5 22.0 %all-to-all-start.2 = ((bf16[32,2,8,512]{3,2,1,0:T(8,128)(2,1)}), bf16[32,2,8,512]{3,2,1,0:T(8,128)(2,1)S(1)}, u32[]{:S(2)}, u32[]{:S(2)}) async-start(bf16[32,2,8,512]{3,2,1,0:T(8,128)(2,1)} %stack.27), calls=%async_computation.2 | async-start | bytes 1048576 | tf_op jit(solution)/shard_map/all_to_all | solution.py:90
  58.8 6.4 %collective-permute-start.2 = (bf16[2,8,512]{2,1,0:T(8,128)(2,1)S(1)}, bf16[2,8,512]{2,1,0:T(8,128)(2,1)S(1)}, u32[]{:S(2)}, u32[]{:S(2)}) collective-permute-start(bf16[2,8,512]{2,1,0:T(8,128)(2,1)S(1)} %collective-permute-done.1), channel_id=1, source_target_pairs={{0,32},{32,64},{64,96},{96,128},{128,160},{160,192},{192,224},{224... | collective-permute-start | bytes 49160 | tf_op jit(solution)/shard_map/ppermute | solution.py:13
  75.6 33.4 %copy-start.12 = (bf16[32,2,8,512]{3,2,1,0:T(8,128)(2,1)}, bf16[32,2,8,512]{3,2,1,0:T(8,128)(2,1)S(1)}, u32[]{:S(2)}) copy-start(bf16[32,2,8,512]{3,2,1,0:T(8,128)(2,1)S(1)} %all-to-all-done.2) | copy-start | bytes 1572868
  76.5 21.9 %all-to-all-start.3 = ((bf16[32,2,8,512]{3,2,1,0:T(8,128)(2,1)}), bf16[32,2,8,512]{3,2,1,0:T(8,128)(2,1)S(1)}, u32[]{:S(2)}, u32[]{:S(2)}) async-start(bf16[32,2,8,512]{3,2,1,0:T(8,128)(2,1)} %stack.28), calls=%async_computation.3 | async-start | bytes 1048576 | tf_op jit(solution)/shard_map/all_to_all | solution.py:90
  81.7 6.3 %collective-permute-start.3 = (bf16[2,8,512]{2,1,0:T(8,128)(2,1)S(1)}, bf16[2,8,512]{2,1,0:T(8,128)(2,1)S(1)}, u32[]{:S(2)}, u32[]{:S(2)}) collective-permute-start(bf16[2,8,512]{2,1,0:T(8,128)(2,1)S(1)} %collective-permute-done.2), channel_id=1, source_target_pairs={{0,32},{32,64},{64,96},{96,128},{128,160},{160,192},{192,224},{224... | collective-permute-start | bytes 49160 | tf_op jit(solution)/shard_map/ppermute | solution.py:13
  88.0 17.0 %collective-permute-start.4 = (bf16[2,8,512]{2,1,0:T(8,128)(2,1)S(1)}, bf16[2,8,512]{2,1,0:T(8,128)(2,1)S(1)}, u32[]{:S(2)}, u32[]{:S(2)}) collective-permute-start(bf16[2,8,512]{2,1,0:T(8,128)(2,1)S(1)} %collective-permute-done.3), channel_id=1, source_target_pairs={{0,32},{32,64},{64,96},{96,128},{128,160},{160,192},{192,224},{224... | collective-permute-start | bytes 49160 | tf_op jit(solution)/shard_map/ppermute | solution.py:13
  98.4 16.1 %copy-start.14 = (bf16[32,2,8,512]{3,2,1,0:T(8,128)(2,1)}, bf16[32,2,8,512]{3,2,1,0:T(8,128)(2,1)S(1)}, u32[]{:S(2)}) copy-start(bf16[32,2,8,512]{3,2,1,0:T(8,128)(2,1)S(1)} %all-to-all-done.3) | copy-start | bytes 1572868
  99.3 22.6 %all-to-all-start.4 = ((bf16[32,2,8,512]{3,2,1,0:T(8,128)(2,1)}), bf16[32,2,8,512]{3,2,1,0:T(8,128)(2,1)}, u32[]{:S(2)}, u32[]{:S(2)}) async-start(bf16[32,2,8,512]{3,2,1,0:T(8,128)(2,1)} %stack.29), calls=%async_computation.4 | async-start | bytes 1048576 | tf_op jit(solution)/shard_map/all_to_all | solution.py:90
  105.0 8.1 %collective-permute-start.5 = (bf16[2,8,512]{2,1,0:T(8,128)(2,1)S(1)}, bf16[2,8,512]{2,1,0:T(8,128)(2,1)S(1)}, u32[]{:S(2)}, u32[]{:S(2)}) collective-permute-start(bf16[2,8,512]{2,1,0:T(8,128)(2,1)S(1)} %collective-permute-done.4), channel_id=1, source_target_pairs={{0,32},{32,64},{64,96},{96,128},{128,160},{160,192},{192,224},{224... | collective-permute-start | bytes 49160 | tf_op jit(solution)/shard_map/ppermute | solution.py:13
  108.1 20.9 %copy-start.20 = (bf16[256,512]{0,1:T(8,128)(2,1)}, bf16[256,512]{0,1:T(8,128)(2,1)S(1)}, u32[]{:S(2)}) copy-start(bf16[256,512]{0,1:T(8,128)(2,1)S(1)} %copy.108) | copy-start | bytes 786436
  113.1 50.0 %collective-permute-start.6 = (bf16[2,8,512]{2,1,0:T(8,128)(2,1)S(1)}, bf16[2,8,512]{2,1,0:T(8,128)(2,1)}, u32[]{:S(2)}, u32[]{:S(2)}) collective-permute-start(bf16[2,8,512]{2,1,0:T(8,128)(2,1)S(1)} %collective-permute-done.5), channel_id=1, source_target_pairs={{0,32},{32,64},{64,96},{96,128},{128,160},{160,192},{192,224},{224... | collective-permute-start | bytes 49160 | tf_op jit(solution)/shard_map/ppermute | solution.py:13
  122.9 23.0 %all-to-all-start.5 = ((bf16[32,2,8,512]{3,2,1,0:T(8,128)(2,1)}), bf16[32,2,8,512]{3,2,1,0:T(8,128)(2,1)}, u32[]{:S(2)}, u32[]{:S(2)}) async-start(bf16[32,2,8,512]{3,2,1,0:T(8,128)(2,1)} %stack.30), calls=%async_computation.5 | async-start | bytes 1048576 | tf_op jit(solution)/shard_map/all_to_all | solution.py:90
  134.5 2.9 %copy-start.15 = (bf16[32,2,8,512]{3,2,1,0:T(8,128)(2,1)S(1)}, bf16[32,2,8,512]{3,2,1,0:T(8,128)(2,1)}, u32[]{:S(2)}) copy-start(bf16[32,2,8,512]{3,2,1,0:T(8,128)(2,1)} %copy-done.14) | copy-start | bytes 1572868
  146.7 22.8 %all-to-all-start.6 = ((bf16[32,2,8,512]{3,2,1,0:T(8,128)(2,1)}), bf16[32,2,8,512]{3,2,1,0:T(8,128)(2,1)}, u32[]{:S(2)}, u32[]{:S(2)}) async-start(bf16[32,2,8,512]{3,2,1,0:T(8,128)(2,1)} %stack.31), calls=%async_computation.6 | async-start | bytes 1048576 | tf_op jit(solution)/shard_map/all_to_all | solution.py:90
  171.1 22.6 %all-to-all-start.7 = ((bf16[32,2,8,512]{3,2,1,0:T(8,128)(2,1)}), bf16[32,2,8,512]{3,2,1,0:T(8,128)(2,1)}, u32[]{:S(2)}, u32[]{:S(2)}) async-start(bf16[32,2,8,512]{3,2,1,0:T(8,128)(2,1)} %stack.32), calls=%async_computation.7 | async-start | bytes 1048576 | tf_op jit(solution)/shard_map/all_to_all | solution.py:90
  198.7 1.8 copy-start.6
  200.8 2.0 copy-start.2
  202.1 1.7 copy-start.3
  202.8 1.7 copy-start.4
  203.8 1.7 copy-start.5
  211.1 13.3 %slice-start = ((s8[4718592]{0:T(1024)(128)(4,1)}), s8[4194304]{0:T(1024)(128)(4,1)S(1)}, s32[]{:S(2)}) async-start(s8[4718592]{0:T(1024)(128)(4,1)} %bitcast.343), calls=%async_computation.8 | async-start | bytes 8388608
  212.8 11.7 %slice-start.1 = ((s8[4718592]{0:T(1024)(128)(4,1)}), s8[524288]{0:T(1024)(128)(4,1)S(1)}, s32[]{:S(2)}) async-start(s8[4718592]{0:T(1024)(128)(4,1)} %bitcast.343), calls=%async_computation.9 | async-start | bytes 1048576
  213.4 6.2 %collective-permute-start.7 = (bf16[1,128,512]{2,1,0:T(8,128)(2,1)S(1)}, bf16[1,128,512]{2,1,0:T(8,128)(2,1)S(1)}, u32[]{:S(2)}, u32[]{:S(2)}) collective-permute-start(bf16[1,128,512]{2,1,0:T(8,128)(2,1)S(1)} %get-tuple-element.63), channel_id=1, source_target_pairs={{0,1},{1,2},{2,3},{3,4},{4,5},{5,6},{6,7},{7,8},{8,9},{9,10},{10,1... | collective-permute-start | bytes 393224 | tf_op jit(solution)/shard_map/ppermute | solution.py:21
  217.6 6.3 %collective-permute-start.8 = (bf16[1,128,512]{2,1,0:T(8,128)(2,1)S(1)}, bf16[1,128,512]{2,1,0:T(8,128)(2,1)S(1)}, u32[]{:S(2)}, u32[]{:S(2)}) collective-permute-start(bf16[1,128,512]{2,1,0:T(8,128)(2,1)S(1)} %get-tuple-element.62), channel_id=1, source_target_pairs={{1,0},{2,1},{3,2},{4,3},{5,4},{6,5},{7,6},{8,7},{9,8},{10,9},{11,1... | collective-permute-start | bytes 393224 | tf_op jit(solution)/shard_map/ppermute | solution.py:24
  (10 other events, 11.8 us)
